TPU v7x, 256 devices: a whole 4x4x8 slice. The times are simulated.
256 devices in a mesh: mod: 16 (over z, y_lo), pulse: 16 (over y_hi, x, core).
Axes of the slice: x: 4, y: 4 (y_hi: 2, y_lo: 2; y = y_hi * 2 + y_lo), z: 8, core: 2. Of those that a mesh axis runs over, the one named last changes fastest.
Arguments:
- raw_frames: bfloat16 [16, 16, 16, 128, 512], P('pulse', None, 'mod'), may hold values from -6 to 6
- gain_section: int32 [16, 16, 16, 16, 512], P('pulse', None, 'mod'), may hold values from 0 to 6560, as said below
- offset: float32 [16, 3, 128, 512], P('mod'), may hold values from -3 to 3
- gain_factor: float32 [16, 3, 128, 512], P('mod'), may hold values from 0.5 to 2
- row_map: bfloat16 [1024, 1024], replicated, as said below
- column_map: bfloat16 [1024, 1024], replicated
- reference_image: bfloat16 [1024, 1024], P(('mod', 'pulse')), may hold values from -6 to 6
- shifts: int32 [2, 16, 16, 64], P(None, 'pulse', 'mod'), may hold values from -24 to 24
Outputs:
- scores: float32 [16, 16, 64], P('pulse', 'mod')
- new_reference: float32 [1024, 1024], P(('mod', 'pulse'))
Inputs may be any that keep to these rules, and one draw needn't show every extreme that they name: `gain_section`: each word holds the gain sections 0, 1 or 2 of 8 consecutive pixel rows in base 3, row 8 p + k as the digit of 3 ** k. row_map and column_map are the identity plus a dense interpolation part.
All inputs are finite; a program needn't handle non-finite values.
Results may differ from a plain program's by a relative error of at most 0.0005.
The roundings to bfloat16 on the way count: a program that leaves them out, or rounds other values in their place, can miss the bound.
Values may be sent and summed in bfloat16 or wider, within the bound.
A program may use at most 128 MiB of HBM per device.

v0:
```python
import jax
import jax.numpy as jnp
from jax import lax
from jax.sharding import PartitionSpec as P

MR = 128
MC = 512
TS = 128
SH = 24
TILES = 64
prior_weight = 16.0


def unpack_section(packed):
    powers = jnp.array([1, 3, 9, 27, 81, 243, 729, 2187], dtype=jnp.int32)
    section = jnp.remainder(jnp.floor_divide(packed[..., :, None, :], powers[:, None]), 3)
    return section.reshape(packed.shape[:-2] + (packed.shape[-2] * 8, packed.shape[-1]))


def calibrate(raw_frames, gain_section, offset, gain_factor):
    dark_level = jnp.where(
        gain_section == 0, offset[:, 0], jnp.where(gain_section == 1, offset[:, 1], offset[:, 2])
    )
    factor = jnp.where(
        gain_section == 0,
        gain_factor[:, 0],
        jnp.where(gain_section == 1, gain_factor[:, 1], gain_factor[:, 2]),
    )
    return ((raw_frames.astype(jnp.float32) - dark_level) * factor).astype(jnp.bfloat16)


def assemble(modules_now):
    quadrants = modules_now.reshape(2, 2, 4, MR, MC)
    return quadrants.transpose(0, 2, 3, 1, 4).reshape(8 * MR, 2 * MC)


def frame_image(modules_now, row_map, column_map):
    assembled = assemble(modules_now)
    row_mapped = jnp.dot(row_map, assembled, preferred_element_type=jnp.float32).astype(
        jnp.bfloat16
    )
    return jnp.dot(row_mapped, column_map, preferred_element_type=jnp.float32).astype(jnp.bfloat16)


def track_tiles(lab_image, ref_padded, shift_rows, shift_cols, splat_map, cover_map):
    tiles_across = lab_image.shape[1] // TS
    tiles_count = lab_image.shape[0] // TS * tiles_across

    def tile_step(index, carried):
        splat_map, cover_map, scores = carried
        index = jnp.asarray(index).astype(jnp.int32)
        row_start = index // tiles_across * TS
        col_start = index % tiles_across * TS
        top_edge = row_start + shift_rows[index] + SH
        left_edge = col_start + shift_cols[index] + SH
        frame_tile = lax.dynamic_slice(lab_image, (row_start, col_start), (TS, TS)).astype(
            jnp.float32
        )
        window = lax.dynamic_slice(ref_padded, (top_edge, left_edge), (TS, TS)).astype(jnp.float32)
        score_value = jnp.sum(frame_tile * window) / TS
        weight = jax.nn.sigmoid(score_value)
        current = lax.dynamic_slice(splat_map, (top_edge, left_edge), (TS, TS))
        splat_map = lax.dynamic_update_slice(
            splat_map, current + weight * frame_tile, (top_edge, left_edge)
        )
        scores = scores.at[index].set(score_value)
        return (splat_map, cover_map, scores)

    start = (splat_map, cover_map, jnp.zeros((tiles_count,), jnp.float32))
    return lax.fori_loop(0, tiles_count, tile_step, start)


def reduce_single(splat_map):
    return lax.psum_scatter(splat_map, ("mod", "pulse"), scatter_dimension=0, tiled=True)


def recount(scores, shift_rows, shift_cols, height, width):
    weights = jax.nn.sigmoid(scores)
    all_weights, all_rows, all_cols = (
        lax.all_gather(weights, ("mod", "pulse"), axis=0, tiled=True),
        lax.all_gather(shift_rows.astype(jnp.float32), ("mod", "pulse"), axis=0, tiled=True),
        lax.all_gather(shift_cols.astype(jnp.float32), ("mod", "pulse"), axis=0, tiled=True),
    )
    tiles_across = width // TS
    tile_index = jnp.arange(TILES)
    base_rows = (tile_index // tiles_across * TS).astype(jnp.float32)
    base_cols = (tile_index % tiles_across * TS).astype(jnp.float32)
    group_size = 32
    block_count = all_weights.shape[0] // group_size
    block_width = group_size * TILES
    weight_blocks = all_weights.reshape(block_count, block_width)
    top_blocks = (all_rows + base_rows[None, :]).reshape(block_count, block_width)
    left_blocks = (all_cols + base_cols[None, :]).reshape(block_count, block_width)
    row_count = height // (lax.axis_size("mod") * lax.axis_size("pulse"))
    owner_index = lax.axis_index("mod") * lax.axis_size("pulse") + lax.axis_index("pulse")
    owner_rows = (owner_index * row_count + jnp.arange(row_count)).astype(jnp.float32)
    all_columns = jnp.arange(width).astype(jnp.float32)

    def add_block(running, block):
        weight_now, top_now, left_now = block
        row_hit = (
            (owner_rows[:, None] >= top_now[None, :])
            & (owner_rows[:, None] < top_now[None, :] + TS)
        ).astype(jnp.float32)
        col_hit = (
            (all_columns[None, :] >= left_now[:, None])
            & (all_columns[None, :] < left_now[:, None] + TS)
        ).astype(jnp.float32)
        product = jnp.dot(
            row_hit * weight_now[None, :],
            col_hit,
            precision=lax.Precision.HIGHEST,
            preferred_element_type=jnp.float32,
        )
        return (running + product, None)

    empty = jnp.zeros((row_count, width), jnp.float32)
    return lax.scan(add_block, empty, (weight_blocks, top_blocks, left_blocks))[0]


def per_device(
    raw_frames, gain_section, offset, gain_factor, row_map, column_map, reference_image, shifts
):
    calibrated = calibrate(raw_frames, unpack_section(gain_section), offset, gain_factor)
    regrouped = lax.all_to_all(calibrated, "mod", split_axis=1, concat_axis=2, tiled=True)
    whole_reference = lax.all_gather(reference_image, ("mod", "pulse"), axis=0, tiled=True)
    height = 8 * MR
    width = 2 * MC
    ref_padded = jnp.pad(whole_reference, SH)
    empty = jnp.zeros((height + 2 * SH, width + 2 * SH), jnp.float32)
    frames = regrouped[0]
    shift_rows = shifts[0, 0]
    shift_cols = shifts[1, 0]

    def per_frame(carried, inputs):
        modules_now, rows_now, cols_now = inputs
        lab_image = frame_image(modules_now, row_map, column_map)
        splat_map, cover_map, scores = track_tiles(
            lab_image, ref_padded, rows_now, cols_now, carried[0], carried[1]
        )
        return ((splat_map, cover_map), scores)

    (splat_map, cover_map), scores = lax.scan(
        per_frame, (empty, empty), (frames, shift_rows, shift_cols)
    )
    splat_map = splat_map[SH : SH + height, SH : SH + width]
    owned_splat = reduce_single(splat_map)
    owned_cover = recount(scores, shift_rows, shift_cols, height, width)
    new_reference = (owned_splat + prior_weight * reference_image.astype(jnp.float32)) / (
        owned_cover + prior_weight
    )
    return (scores.reshape(1, scores.shape[0], scores.shape[1]), new_reference)


def solution(mesh):
    return jax.shard_map(
        per_device,
        mesh=mesh,
        in_specs=(
            P("pulse", None, "mod", None, None),
            P("pulse", None, "mod", None, None),
            P("mod", None, None, None),
            P("mod", None, None, None),
            P(),
            P(),
            P(("mod", "pulse"), None),
            P(None, "pulse", "mod", None),
        ),
        out_specs=(P("pulse", "mod", None), P(("mod", "pulse"), None)),
        check_vma=False,
    )
```

profile of v0, /device:TPU:1, one launch (start us, length us, event | category | flops | bytes accessed | tf_op | source)
XLA Modules:
  0.0 1815.0 jit_solution(10373691381890550767)
XLA Ops:
  11.3 46.8 %multiply_convert_fusion = bf16[1,16,1,128,512]{4,3,2,0,1:T(8,128)(2,1)} fusion(bf16[1,16,1,128,512]{4,3,2,1,0:T(8,128)(2,1)S(1)} %copy-done.1, f32[128,512]{1,0:T(8,128)S(1)} %get-tuple-element.391, f32[128,512]{1,0:T(8,128)S(1)} %get-tuple-element.392, f32[128,512]{1,0:T(8,128)S(1)} %get-tuple-element.390, f32[128,512]{1,0:T(8,128)S(1)} %get-tuple-element.398, ...), kind=kLoop, calls=%fused_computation.36 | loop fusion | flops 23068672 | bytes 6423040 | tf_op jit(solution)/shard_map/convert_element_type | solution.py:29
  58.1 10.2 all-to-all-start
  69.3 47.6 %all-to-all-done = bf16[1,16,1,128,512]{4,3,2,0,1:T(8,128)(2,1)} async-done(((bf16[1,16,1,128,512]{4,3,2,0,1:T(8,128)(2,1)}), bf16[1,16,1,128,512]{4,3,2,0,1:T(8,128)(2,1)}, u32[]{:S(2)}, u32[]{:S(2)}) %all-to-all-start) | async-done | bytes 2097184 | tf_op jit(solution)/shard_map/all_to_all | solution.py:125
  117.0 3.8 copy.13
  122.6 8.2 fusion.26
  130.8 360.6 %all-gather.6.cloned.1.call-done = bf16[256,4,1024]{2,1,0:T(4,128)(2,1)} async-done(((bf16[1,4,1024]{2,1,0:T(4,128)(2,1)}), bf16[256,4,1024]{2,1,0:T(4,128)(2,1)}) %all-gather.6.cloned.1.call-update) | async-done | bytes 2097168 | tf_op jit(solution)/shard_map/all_gather | solution.py:126
  491.5 4.0 reshape.340
  495.4 4.2 pad.8
  502.2 589.1 %while.40 = (s32[]{:T(128)}, f32[1072,1072]{1,0:T(8,128)}, f32[64]{0:T(128)S(1)}, s32[64]{0:T(128)S(1)}, s32[64]{0:T(128)S(1)}, /*index=5*/bf16[1024,1024]{1,0:T...) while((s32[]{:T(128)}, f32[1072,1072]{1,0:T(8,128)}, ...), condition=%wide.region_2.3_spmd, body=%wide.region_0.2_spmd.sunk | while | flops 114727 | bytes 361614 | solution.py:70
  508.0 3.3 dynamic_update_slice.15
  517.3 3.2 dynamic_update_slice.15
  526.5 3.3 dynamic_update_slice.15
  535.7 3.2 dynamic_update_slice.15
  563.2 3.2 dynamic_update_slice.15
  572.5 3.2 dynamic_update_slice.15
  590.9 3.2 dynamic_update_slice.15
  609.3 3.2 dynamic_update_slice.15
  627.8 3.3 dynamic_update_slice.15
  637.0 3.2 dynamic_update_slice.15
  646.3 3.2 dynamic_update_slice.15
  673.9 3.3 dynamic_update_slice.15
  683.2 3.2 dynamic_update_slice.15
  692.4 3.2 dynamic_update_slice.15
  701.6 3.2 dynamic_update_slice.15
  710.9 3.2 dynamic_update_slice.15
  766.2 3.3 dynamic_update_slice.15
  775.4 3.3 dynamic_update_slice.15
  784.7 3.2 dynamic_update_slice.15
  793.9 3.3 dynamic_update_slice.15
  812.4 3.2 dynamic_update_slice.15
  830.8 3.2 dynamic_update_slice.15
  840.0 3.2 dynamic_update_slice.15
  849.3 3.3 dynamic_update_slice.15
  858.5 3.2 dynamic_update_slice.15
  867.7 3.2 dynamic_update_slice.15
  877.0 3.2 dynamic_update_slice.15
  895.4 3.3 dynamic_update_slice.15
  913.9 3.3 dynamic_update_slice.15
  923.2 3.2 dynamic_update_slice.15
  941.6 3.2 dynamic_update_slice.15
  960.1 3.2 dynamic_update_slice.15
  978.5 3.2 dynamic_update_slice.15
  987.7 3.2 dynamic_update_slice.15
  1015.4 3.3 dynamic_update_slice.15
  1091.3 5.5 slice.52
  1097.6 343.4 %all-gather = f32[256,1,1,64]{3,2,1,0:T(1,128)S(1)} all-gather(f32[1,1,1,64]{3,2,1,0:T(1,128)S(1)} %get-tuple-element.394), channel_id=2, replica_groups=mesh['mod'=16,'pulse'=16] {'mod','pulse'}, dimensions={0}, use_global_device_ids=true | all-gather | bytes 65792 | tf_op jit(solution)/shard_map/all_gather | solution.py:81
  1441.2 339.5 %all-gather.2 = f32[256,1,1,64]{3,2,1,0:T(1,128)S(1)} all-gather(f32[1,1,1,64]{3,2,1,0:T(1,128)S(1)} %get-tuple-element.393), channel_id=4, replica_groups=mesh['mod'=16,'pulse'=16] {'mod','pulse'}, dimensions={0}, use_global_device_ids=true | all-gather | bytes 65792 | tf_op jit(solution)/shard_map/all_gather | solution.py:82
  1781.7 25.1 %while.41 = (s32[]{:T(128)}, f32[4,1024]{1,0:T(4,128)S(1)}, f32[8,2048]{1,0:T(8,128)S(1)}, f32[8,2048]{1,0:T(8,128)S(1)}, f32[8,2048]{1,0:T(8,128)S(1)}, /*index=5*/s32[]{:T(128)}, s32[]{:T(128)}, s32[]{:T(128)}) while((s32[]{:T(128)}, f32[4,1024]{1,0:T(4,128)S(1)}, f32[8,2048]{1,0:T(8,128)S(1)}, ...), condition=%wide.region_5.6_spmd.clone.clone, body=%wide.region_4.5_spmd.clone.clone.sunk | while | flops 107000840 | bytes 155787 | solution.py:118
  (433 shorter events, 381.7 us)
Async XLA Ops:
  7.2 115.4 %copy-start = (bf16[1024,1024]{1,0:T(8,128)(2,1)S(1)}, bf16[1024,1024]{1,0:T(8,128)(2,1)}, u32[]{:S(2)}) copy-start(bf16[1024,1024]{1,0:T(8,128)(2,1)} %param.20) | copy-start | bytes 6291460
  9.3 2.1 copy-start.1
  11.3 58.0 %copy-start.5 = (s32[2,1,1,64]{3,2,1,0:T(1,128)S(1)}, s32[2,1,1,64]{3,2,1,0:T(1,128)}, u32[]{:S(2)}) copy-start(s32[2,1,1,64]{3,2,1,0:T(1,128)} %param.22) | copy-start | bytes 1540
  58.1 58.8 %all-to-all-start = ((bf16[1,16,1,128,512]{4,3,2,0,1:T(8,128)(2,1)}), bf16[1,16,1,128,512]{4,3,2,0,1:T(8,128)(2,1)}, u32[]{:S(2)}, u32[]{:S(2)}) async-start(bf16[1,16,1,128,512]{4,3,2,0,1:T(8,128)(2,1)} %multiply_convert_fusion), calls=%async_computation | async-start | bytes 4194304 | tf_op jit(solution)/shard_map/all_to_all | solution.py:125
  68.3 423.1 %all-gather.6.cloned.1.call-start = ((), (), s32[]{:S(2)}) async-start(), calls=%async_computation.1 | async-start | bytes 2105344 | tf_op jit(solution)/shard_map/all_gather | solution.py:126
  69.1 1711.7 %all-reduce.6.cloned.1.call-start = ((), (), s32[]{:S(2)}) async-start(), calls=%async_computation.2 | async-start | bytes 8519680
  1091.3 5.5 copy-start.4
  1096.9 0.6 copy-start.2
  1781.7 25.2 %copy-start.3 = (bf16[4,1024]{1,0:T(4,128)(2,1)S(1)}, bf16[4,1024]{1,0:T(4,128)(2,1)}, u32[]{:S(2)}) copy-start(bf16[4,1024]{1,0:T(4,128)(2,1)} %param.21) | copy-start | bytes 24580
Sparse Core Ops, SparseCore 0:
  71.0 420.3 all-gather.5
  1097.7 271.1 all-reduce.5
where the time goes:
time: 1830 us; the launch traced here: 1820 us
  blocking collectives  683 us (37%)
  waiting for transfers between devices  409 us (22%)
  local copies, waits for them, and re-layouts  307 us (17%)
  other arithmetic  227 us (12%)
  loops' own time  132 us (7%)
  matrix products  32.6 us (2%)
    all_gather x1, waiting for transfers between devices, per_device(): lax.all_gather(reference_image, ('mod', 'pulse'), axis=0, tiled=True)  361 us
    all_gather x1, blocking collectives, recount(): lax.all_gather(shift_rows.astype(jnp.float32), ('mod', 'pulse'), axis=0,...  343 us
    all_gather x1, blocking collectives, recount(): lax.all_gather(shift_cols.astype(jnp.float32), ('mod', 'pulse'), axis=0,...  339 us
    dynamic_update_slice x64, local copies, waits for them, and re-layouts, tile_step(): lax.dynamic_update_slice(splat_map, current + weight * frame_tile, (top_e...  206 us
    another operation x1, loops' own time, track_tiles(): return lax.fori_loop(0, tiles_count, tile_step, start)  131 us
    reduce_sum x64, other arithmetic, tile_step(): score_value = jnp.sum(frame_tile * window) / TS  102 us
    add x64, other arithmetic, tile_step(): current + weight * frame_tile  65 us
    all_to_all x1, waiting for transfers between devices, per_device(): lax.all_to_all(calibrated, 'mod', split_axis=1, concat_axis=2, tiled=True)  47.6 us
  transfers between devices with their start and end apart: 3, of which 2 were waited for; matrix products, arithmetic and copies ran while one was open for 1% of the time, Pallas kernels for 0%

commit v1 on v0

--- a/solution.py
+++ b/solution.py
@@ -9,6 +9,13 @@
 SH = 24
 TILES = 64
 prior_weight = 16.0
+
+
+def _handle_skins(x0, group_axis, array_dim=0):
+    z1 = jax.lax.axis_size(group_axis)
+    res = jnp.stack(z1 * [x0], axis=0)
+    after = jax.lax.all_to_all(res, axis_name=group_axis, split_axis=0, concat_axis=0)
+    return jnp.concatenate(after, array_dim)
 
 
 def unpack_section(packed):
@@ -78,7 +85,7 @@
     weights = jax.nn.sigmoid(scores)
     all_weights, all_rows, all_cols = (
         lax.all_gather(weights, ("mod", "pulse"), axis=0, tiled=True),
-        lax.all_gather(shift_rows.astype(jnp.float32), ("mod", "pulse"), axis=0, tiled=True),
+        _handle_skins(shift_rows.astype(jnp.float32), ("mod", "pulse")),
         lax.all_gather(shift_cols.astype(jnp.float32), ("mod", "pulse"), axis=0, tiled=True),
     )
     tiles_across = width // TS

time: 1830 us -> 1510 us (0.83)
  blocking collectives: 683 us -> 348 us
    all_gather x1 -> x0, blocking collectives: 343 us -> none  [recount(): lax.all_gather(shift_rows.astype(jnp.float32), ('mod', 'pulse'), axis=0,...]
  transfers between devices with their start and end apart: 3 -> 4, of which waited for: 2 -> 2; matrix products, arithmetic and copies ran while one was open for 1% -> 1% of each run, Pallas kernels for 0% -> 0%
where the time goes in v1:
time: 1510 us; the launch traced here: 1490 us
  waiting for transfers between devices  409 us (27%)
  blocking collectives  348 us (23%)
  local copies, waits for them, and re-layouts  308 us (20%)
  other arithmetic  228 us (15%)
  loops' own time  132 us (9%)
  matrix products  32.6 us (2%)
  starting transfers between devices  22.8 us (2%)
    all_gather x1, waiting for transfers between devices, per_device(): lax.all_gather(reference_image, ('mod', 'pulse'), axis=0, tiled=True)  361 us
    all_gather x1, blocking collectives, recount(): lax.all_gather(shift_cols.astype(jnp.float32), ('mod', 'pulse'), axis=0,...  348 us
    dynamic_update_slice x64, local copies, waits for them, and re-layouts, tile_step(): lax.dynamic_update_slice(splat_map, current + weight * frame_tile, (top_e...  205 us
    another operation x1, loops' own time, track_tiles(): return lax.fori_loop(0, tiles_count, tile_step, start)  131 us
    reduce_sum x64, other arithmetic, tile_step(): score_value = jnp.sum(frame_tile * window) / TS  102 us
    add x64, other arithmetic, tile_step(): current + weight * frame_tile  65 us
    all_to_all x1, waiting for transfers between devices, per_device(): lax.all_to_all(calibrated, 'mod', split_axis=1, concat_axis=2, tiled=True)  47.6 us
    convert_element_type x1, other arithmetic, calibrate(): ((raw_frames.astype(jnp.float32) - dark_level) * factor).astype(jnp.bfloa...  46.8 us
  transfers between devices with their start and end apart: 4, of which 2 were waited for; matrix products, arithmetic and copies ran while one was open for 1% of the time, Pallas kernels for 0%

profile of v1, /device:TPU:1, one launch (start us, length us, event | category | flops | bytes accessed | tf_op | source)
XLA Modules:
  0.0 1494.9 jit_solution(4668315285427713560)
XLA Ops:
  11.3 46.8 %multiply_convert_fusion = bf16[1,16,1,128,512]{4,3,2,0,1:T(8,128)(2,1)} fusion(bf16[1,16,1,128,512]{4,3,2,1,0:T(8,128)(2,1)S(1)} %copy-done.1, f32[128,512]{1,0:T(8,128)S(1)} %get-tuple-element.391, f32[128,512]{1,0:T(8,128)S(1)} %get-tuple-element.392, f32[128,512]{1,0:T(8,128)S(1)} %get-tuple-element.390, f32[128,512]{1,0:T(8,128)S(1)} %get-tuple-element.398, ...), kind=kLoop, calls=%fused_computation.36 | loop fusion | flops 23068672 | bytes 6423040 | tf_op jit(solution)/shard_map/convert_element_type | solution.py:36
  58.2 10.2 all-to-all-start
  69.3 47.6 %all-to-all-done = bf16[1,16,1,128,512]{4,3,2,0,1:T(8,128)(2,1)} async-done(((bf16[1,16,1,128,512]{4,3,2,0,1:T(8,128)(2,1)}), bf16[1,16,1,128,512]{4,3,2,0,1:T(8,128)(2,1)}, u32[]{:S(2)}, u32[]{:S(2)}) %all-to-all-start) | async-done | bytes 2097184 | tf_op jit(solution)/shard_map/all_to_all | solution.py:132
  117.0 3.8 copy.13
  122.6 8.2 fusion.26
  130.8 360.6 %all-gather.5.cloned.1.call-done = bf16[256,4,1024]{2,1,0:T(4,128)(2,1)} async-done(((bf16[1,4,1024]{2,1,0:T(4,128)(2,1)}), bf16[256,4,1024]{2,1,0:T(4,128)(2,1)}) %all-gather.5.cloned.1.call-update) | async-done | bytes 2097168 | tf_op jit(solution)/shard_map/all_gather | solution.py:133
  491.5 3.9 reshape.340
  495.4 4.2 pad.8
  502.2 589.0 %while.40 = (s32[]{:T(128)}, f32[1072,1072]{1,0:T(8,128)}, f32[64]{0:T(128)S(1)}, s32[64]{0:T(128)S(1)}, s32[64]{0:T(128)S(1)}, /*index=5*/bf16[1024,1024]{1,0:T...) while((s32[]{:T(128)}, f32[1072,1072]{1,0:T(8,128)}, ...), condition=%wide.region_2.3_spmd, body=%wide.region_0.2_spmd.sunk | while | flops 114727 | bytes 361614 | solution.py:77
  508.0 3.2 dynamic_update_slice.15
  526.5 3.2 dynamic_update_slice.15
  535.7 3.2 dynamic_update_slice.15
  563.2 3.3 dynamic_update_slice.15
  572.4 3.2 dynamic_update_slice.15
  581.7 3.3 dynamic_update_slice.15
  600.1 3.2 dynamic_update_slice.15
  609.4 3.2 dynamic_update_slice.15
  627.8 3.2 dynamic_update_slice.15
  646.2 3.3 dynamic_update_slice.15
  655.5 3.2 dynamic_update_slice.15
  664.7 3.3 dynamic_update_slice.15
  673.9 3.2 dynamic_update_slice.15
  692.4 3.2 dynamic_update_slice.15
  720.0 3.2 dynamic_update_slice.15
  729.3 3.3 dynamic_update_slice.15
  738.5 3.3 dynamic_update_slice.15
  747.8 3.3 dynamic_update_slice.15
  757.0 3.3 dynamic_update_slice.15
  803.1 3.3 dynamic_update_slice.15
  812.3 3.3 dynamic_update_slice.15
  821.6 3.3 dynamic_update_slice.15
  840.1 3.2 dynamic_update_slice.15
  849.3 3.2 dynamic_update_slice.15
  867.7 3.2 dynamic_update_slice.15
  877.0 3.2 dynamic_update_slice.15
  913.9 3.2 dynamic_update_slice.15
  932.3 3.3 dynamic_update_slice.15
  950.8 3.2 dynamic_update_slice.15
  969.2 3.2 dynamic_update_slice.15
  978.5 3.2 dynamic_update_slice.15
  987.7 3.2 dynamic_update_slice.15
  996.9 3.2 dynamic_update_slice.15
  1006.1 3.2 dynamic_update_slice.15
  1015.4 3.2 dynamic_update_slice.15
  1091.2 5.5 slice.52
  1098.2 12.4 all-to-all-start.1
  1110.7 348.3 %all-gather.1 = f32[256,1,1,64]{3,2,1,0:T(1,128)S(1)} all-gather(f32[1,1,1,64]{3,2,1,0:T(1,128)S(1)} %get-tuple-element.393), channel_id=3, replica_groups=mesh['mod'=16,'pulse'=16] {'mod','pulse'}, dimensions={0}, use_global_device_ids=true | all-gather | bytes 65792 | tf_op jit(solution)/shard_map/all_gather | solution.py:89
  1461.6 25.1 %while.41 = (s32[]{:T(128)}, f32[4,1024]{1,0:T(4,128)S(1)}, f32[8,2048]{1,0:T(8,128)S(1)}, f32[8,2048]{1,0:T(8,128)S(1)}, f32[8,2048]{1,0:T(8,128)S(1)}, /*index=5*/s32[]{:T(128)}, s32[]{:T(128)}, s32[]{:T(128)}) while((s32[]{:T(128)}, f32[4,1024]{1,0:T(4,128)S(1)}, f32[8,2048]{1,0:T(8,128)S(1)}, ...), condition=%wide.region_5.6_spmd.clone.clone, body=%wide.region_4.5_spmd.clone.clone.sunk | while | flops 107000840 | bytes 155787 | solution.py:125
  (439 shorter events, 383.8 us)
Async XLA Ops:
  7.2 115.4 %copy-start = (bf16[1024,1024]{1,0:T(8,128)(2,1)S(1)}, bf16[1024,1024]{1,0:T(8,128)(2,1)}, u32[]{:S(2)}) copy-start(bf16[1024,1024]{1,0:T(8,128)(2,1)} %param.20) | copy-start | bytes 6291460
  9.3 2.1 copy-start.1
  11.3 58.0 %copy-start.5 = (s32[2,1,1,64]{3,2,1,0:T(1,128)S(1)}, s32[2,1,1,64]{3,2,1,0:T(1,128)}, u32[]{:S(2)}) copy-start(s32[2,1,1,64]{3,2,1,0:T(1,128)} %param.22) | copy-start | bytes 1540
  58.2 58.8 %all-to-all-start = ((bf16[1,16,1,128,512]{4,3,2,0,1:T(8,128)(2,1)}), bf16[1,16,1,128,512]{4,3,2,0,1:T(8,128)(2,1)}, u32[]{:S(2)}, u32[]{:S(2)}) async-start(bf16[1,16,1,128,512]{4,3,2,0,1:T(8,128)(2,1)} %multiply_convert_fusion), calls=%async_computation | async-start | bytes 4194304 | tf_op jit(solution)/shard_map/all_to_all | solution.py:132
  68.3 423.1 %all-gather.5.cloned.1.call-start = ((), (), s32[]{:S(2)}) async-start(), calls=%async_computation.2 | async-start | bytes 2105344 | tf_op jit(solution)/shard_map/all_gather | solution.py:133
  69.1 1391.6 %all-reduce.6.cloned.1.call-start = ((), (), s32[]{:S(2)}) async-start(), calls=%async_computation.3 | async-start | bytes 8519680
  1091.2 5.5 copy-start.4
  1096.8 0.6 copy-start.2
  1098.2 361.0 %all-to-all-start.1 = ((f32[256,1,64]{2,1,0:T(1,128)}), f32[256,1,64]{2,1,0:T(1,128)S(1)}, u32[]{:S(2)}, u32[]{:S(2)}) async-start(f32[256,1,64]{2,1,0:T(1,128)} %stack.2), calls=%async_computation.1 | async-start | bytes 262144 | tf_op jit(solution)/shard_map/all_to_all | solution.py:17
  1461.5 25.2 %copy-start.3 = (bf16[4,1024]{1,0:T(4,128)(2,1)S(1)}, bf16[4,1024]{1,0:T(4,128)(2,1)}, u32[]{:S(2)}) copy-start(bf16[4,1024]{1,0:T(4,128)(2,1)} %param.21) | copy-start | bytes 24580
Sparse Core Ops, SparseCore 0:
  71.0 420.3 all-gather.4
  1097.6 271.5 all-reduce.5
